TPU v7x, 32 devices: a whole 2x2x4 slice. The times are simulated.
32 devices in a mesh: seq: 16 (over z, y, x), head: 2 (over core).
Axes of the slice: x: 2, y: 2, z: 4, core: 2. Of those that a mesh axis runs over, the one named last changes fastest.
Arguments:
- tokens: bfloat16 [16, 1024, 3072], P('seq', None, 'head'), may hold values from -6 to 6
- fast_state: float32 [16, 8, 192, 2304], P('seq', 'head'), may hold values from -6 to 6
- momentum: float32 [16, 8, 192, 2304], P('seq', 'head'), may hold values from -1.8 to 1.8
- init_fast: bfloat16 [8, 192, 2304], P('head'), may hold values from -6 to 6
- past_keys: bfloat16 [16, 2048, 1536], P('seq', None, 'head'), may hold values from -6 to 6
- past_values: bfloat16 [16, 2048, 1536], P('seq', None, 'head'), may hold values from -6 to 6
- qkv_weight: bfloat16 [3, 3072, 1536], P(None, 'seq', 'head'), may hold values from -0.109375 to 0.109375
- rate_weight: bfloat16 [3072, 8], P(None, 'head'), may hold values from -0.109375 to 0.109375
- out_weight: bfloat16 [1536, 3072], P('head'), may hold values from -0.15625 to 0.15625
- prompt_begins: int32 [2, 16], replicated, may hold values 0 or 1
Outputs:
- mixed: bfloat16 [16, 1024, 3072], P('seq', None, 'head')
- fast_out: float32 [16, 8, 192, 2304], P('seq', 'head')
- momentum_out: float32 [16, 8, 192, 2304], P('seq', 'head')
All inputs are finite; a program needn't handle non-finite values.
Results may differ from a plain program's by a relative error of at most 0.015.
Values may be sent and summed in bfloat16 or wider, within the bound.
A program may use at most 192 MiB of HBM per device.

v0:
```python
import math
import jax
import jax.numpy as jnp
from jax import lax
from jax.sharding import PartitionSpec as P

SPAN = 512
WINDOW = 2048
STEPS = 2
momentum_decay = 0.9
rate_scale = 0.3
epsilon = 1e-06
highest = lax.Precision.HIGHEST


def passed_along(block, axis, distance):
    devices = range(lax.axis_size(axis))
    route = [((i - distance) % len(devices), i) for i in devices]
    return lax.ppermute(block, axis, route)


def unit_rows(matrix):
    return matrix * lax.rsqrt(jnp.mean(matrix * matrix, axis=-1, keepdims=True) + epsilon)


def head_span(
    queries,
    keys_span,
    values_span,
    step_size,
    window_keys,
    window_values,
    visible_prev,
    restart,
    weights_now,
    momentum_now,
    initial,
):
    span_len = queries.shape[0]
    window_len = window_keys.shape[0]
    head_dim = queries.shape[1]
    hidden = weights_now.shape[1] // 3
    score_bound = math.sqrt(head_dim)
    query_unit = unit_rows(queries.astype(jnp.float32))
    key_unit = unit_rows(keys_span.astype(jnp.float32))
    context_keys = jnp.concatenate(
        [unit_rows(window_keys.astype(jnp.float32)), key_unit], axis=0
    ).astype(jnp.bfloat16)
    context_values = jnp.concatenate([window_values, values_span], axis=0)
    scores = (
        lax.dot_general(
            query_unit.astype(jnp.bfloat16),
            context_keys,
            (((1,), (1,)), ((), ())),
            preferred_element_type=jnp.float32,
        )
        / score_bound
    )
    query_pos = lax.broadcasted_iota(jnp.int32, scores.shape, 0)
    key_pos = lax.broadcasted_iota(jnp.int32, scores.shape, 1)
    restart_flag = restart.astype(jnp.float32)
    keep_prev = jnp.concatenate(
        [visible_prev * (1.0 - restart_flag), jnp.ones((span_len,), jnp.float32)]
    )
    inside = (key_pos > query_pos) & (key_pos <= query_pos + window_len)
    soft_weights = jnp.where(inside, jnp.exp(scores - score_bound), 0.0) * keep_prev[None, :]
    denominator = jnp.sum(soft_weights, axis=1, keepdims=True)
    attended = (
        jnp.dot(
            soft_weights.astype(jnp.bfloat16), context_values, preferred_element_type=jnp.float32
        )
        / denominator
    )
    weights_now = jnp.where(restart > 0, initial.astype(jnp.float32), weights_now)
    momentum_now = jnp.where(restart > 0, jnp.zeros_like(momentum_now), momentum_now)
    up_proj = weights_now[:, : 2 * hidden]
    down_proj = weights_now[:, 2 * hidden :]
    hidden_scale = math.sqrt(hidden)
    query_in = query_unit / score_bound
    key_in = key_unit / score_bound
    both_in = jnp.dot(query_in, up_proj, precision=highest, preferred_element_type=jnp.float32)
    mixed_hidden = jax.nn.silu(both_in[:, :hidden]) * both_in[:, hidden:]
    applied = (
        lax.dot_general(
            mixed_hidden,
            down_proj,
            (((1,), (1,)), ((), ())),
            precision=highest,
            preferred_element_type=jnp.float32,
        )
        / hidden_scale
    )
    both_key = jnp.dot(key_in, up_proj, precision=highest, preferred_element_type=jnp.float32)
    gate_key = both_key[:, :hidden]
    lift_key = both_key[:, hidden:]
    gate_sigmoid = jax.nn.sigmoid(gate_key)
    gate_silu = gate_key * gate_sigmoid
    hidden_key = gate_silu * lift_key
    out_grad = -step_size.astype(jnp.float32)[:, None] * values_span.astype(jnp.float32)
    down_grad = (
        lax.dot_general(
            out_grad,
            hidden_key,
            (((0,), (0,)), ((), ())),
            precision=highest,
            preferred_element_type=jnp.float32,
        )
        / hidden_scale
    )
    hidden_grad = (
        jnp.dot(out_grad, down_proj, precision=highest, preferred_element_type=jnp.float32)
        / hidden_scale
    )
    gate_grad = hidden_grad * lift_key * gate_sigmoid * (1.0 + gate_key * (1.0 - gate_sigmoid))
    lift_grad = hidden_grad * gate_silu
    up_grad = lax.dot_general(
        key_in,
        jnp.concatenate([gate_grad, lift_grad], axis=1),
        (((0,), (0,)), ((), ())),
        precision=highest,
        preferred_element_type=jnp.float32,
    )
    gradient = jnp.concatenate([up_grad, down_grad], axis=1)
    momentum_new = momentum_decay * momentum_now + gradient
    stepped = weights_now - momentum_new
    weights_new = stepped * lax.rsqrt(jnp.mean(stepped * stepped, axis=0, keepdims=True) + epsilon)
    head_mix = (attended + applied).astype(jnp.bfloat16)
    return (head_mix, weights_new, momentum_new)


def position_span(
    queries,
    keys_span,
    values_span,
    step_size,
    window_keys,
    window_values,
    visible_prev,
    restart,
    weights_now,
    momentum_now,
    initial,
):
    heads_here = weights_now.shape[0]

    def split_heads(matrix):
        return matrix.reshape(matrix.shape[0], heads_here, matrix.shape[1] // heads_here)

    mapped = jax.vmap(
        head_span, in_axes=(1, 1, 1, 1, 1, 1, None, None, 0, 0, 0), out_axes=(1, 0, 0)
    )
    head_mix, weights_new, momentum_new = mapped(
        split_heads(queries),
        split_heads(keys_span),
        split_heads(values_span),
        step_size,
        split_heads(window_keys),
        split_heads(window_values),
        visible_prev,
        restart,
        weights_now,
        momentum_now,
        initial,
    )
    return (head_mix.reshape(head_mix.shape[0], -1), weights_new, momentum_new)


def next_window(window_keys, window_values, visible_prev, restart, keys_span, values_span):
    window_len = window_keys.shape[0]
    kept_rows = visible_prev * (1.0 - restart.astype(visible_prev.dtype))
    fresh_rows = jnp.ones((keys_span.shape[0],), visible_prev.dtype)
    new_keys = jnp.concatenate([window_keys, keys_span], axis=0)[-window_len:]
    new_values = jnp.concatenate([window_values, values_span], axis=0)[-window_len:]
    new_visible = jnp.concatenate([kept_rows, fresh_rows])[-window_len:]
    return (new_keys, new_values, new_visible)


def reduce_section(head_mix, out_weight):
    partial_value = jnp.dot(head_mix, out_weight, preferred_element_type=jnp.float32)
    return lax.psum_scatter(
        partial_value.astype(jnp.bfloat16), "head", scatter_dimension=1, tiled=True
    ).astype(jnp.float32)


def body(
    tokens,
    fast_state,
    momentum,
    init_fast,
    past_keys,
    past_values,
    qkv_weight,
    rate_weight,
    out_weight,
    prompt_begins,
):
    position_index = lax.axis_index("seq")
    features = lax.all_gather(tokens[0], "head", axis=1, tiled=True)
    projected = jnp.einsum(
        "tr,crh->cth",
        features,
        lax.all_gather(qkv_weight, "seq", axis=1, tiled=True),
        preferred_element_type=jnp.float32,
    )
    projected_bf = projected.astype(jnp.bfloat16)
    step_sizes = (
        rate_scale
        * jax.nn.softplus(jnp.dot(features, rate_weight, preferred_element_type=jnp.float32))
    ).astype(jnp.bfloat16)
    weights_now = fast_state[0]
    momentum_now = momentum[0]
    window_keys = past_keys[0]
    window_values = past_values[0]
    visible = jnp.ones((WINDOW,), jnp.float32)
    mix_blocks = []
    reduced_parts = []
    for section_index in range(STEPS):
        first_row = section_index * SPAN
        span_bf = projected_bf[:, first_row : first_row + SPAN]
        span_rates = step_sizes[first_row : first_row + SPAN]
        restart = prompt_begins[section_index, position_index]
        head_mix, weights_new, momentum_new = position_span(
            span_bf[0],
            span_bf[1],
            span_bf[2],
            span_rates,
            window_keys,
            window_values,
            visible,
            restart,
            weights_now,
            momentum_now,
            init_fast,
        )
        window_keys, window_values, visible = next_window(
            window_keys, window_values, visible, restart, span_bf[1], span_bf[2]
        )
        if section_index + 1 < STEPS:
            weights_now, momentum_now = (
                passed_along(weights_new.astype(jnp.bfloat16), "seq", 1).astype(weights_new.dtype),
                passed_along(momentum_new.astype(jnp.bfloat16), "seq", 1).astype(
                    momentum_new.dtype
                ),
            )
            window_keys, window_values, visible_wire = passed_along(
                (window_keys, window_values, visible.astype(jnp.bfloat16)), "seq", 1
            )
            visible = visible_wire.astype(jnp.float32)
        else:
            weights_now = weights_new
            momentum_now = momentum_new
        mix_blocks.append(head_mix)
        reduced_parts.append(reduce_section(head_mix, out_weight))
    mixed = jnp.concatenate(reduced_parts, axis=0)
    return (mixed.astype(jnp.bfloat16)[None], weights_now[None], momentum_now[None])


def solution(mesh):
    in_specs = (
        P("seq", None, "head"),
        P("seq", "head", None, None),
        P("seq", "head", None, None),
        P("head", None, None),
        P("seq", None, "head"),
        P("seq", None, "head"),
        P(None, "seq", "head"),
        P(None, "head"),
        P("head", None),
        P(),
    )
    out_specs = (P("seq", None, "head"), P("seq", "head", None, None), P("seq", "head", None, None))
    return jax.shard_map(body, mesh=mesh, in_specs=in_specs, out_specs=out_specs, check_vma=False)
```

profile of v0, /device:TPU:0, one launch (start us, length us, event | category | flops | bytes accessed | tf_op | source)
XLA Modules:
  0.0 601.0 jit_solution(12368685986231815268)
XLA Ops:
  8.7 1.3 constant_dynamic-slice_fusion
  10.7 3.0 collective-permute-start.1
  14.4 5.5 copy.13
  19.9 4.8 multiply_reduce_fusion.3
  24.7 2.0 fusion.44
  26.7 6.9 %convert_select_fusion.1 = f32[4,192,2304]{2,1,0:T(8,128)} fusion(bf16[4,192,2304]{2,1,0:T(8,128)(2,1)S(1)} %copy-done.4, f32[1,4,192,2304]{3,2,1,0:T(8,128)} %param.11, pred[]{:T(512)} %bitcast.21), kind=kLoop, calls=%fused_computation.19 | loop fusion | flops 3538944 | bytes 17694720 | tf_op jit(solution)/shard_map/vmap(jit(_where))/select_n | solution.py:74
  33.6 2.5 multiply_convert_fusion.2
  37.4 3.0 copy.14
  40.4 5.1 fusion.142
  46.2 153.0 %all-gather.4.cloned.1.call-done = bf16[3,3072,768]{2,1,0:T(8,128)(2,1)} async-done(((bf16[3,192,768]{2,1,0:T(8,128)(2,1)}), bf16[3,3072,768]{2,1,0:T(8,128)(2,1)}) %all-gather.4.cloned.1.call-update) | async-done | bytes 14155792 | tf_op jit(solution)/shard_map/all_gather | solution.py:202
  199.2 19.5 %convert_bitcast_fusion = bf16[3,1024,768]{1,2,0:T(8,128)(2,1)S(1)} fusion(bf16[3,3072,768]{2,1,0:T(8,128)(2,1)} %all-gather.4.cloned.1.call-done, bf16[1,1024,3072]{2,1,0:T(8,128)(2,1)} %all-gather.6.cloned.1.call-done), kind=kOutput, calls=%fused_computation.67 | convolution fusion | flops 14497873920 | bytes 25165824 | tf_op jit(solution)/shard_map/tr,crh->cth/dot_general | solution.py:199
  218.7 1.7 fusion.168
  220.7 13.2 %fusion.49 = f32[4,512,1536]{2,1,0:T(8,128)S(1)} fusion(f32[4,192,2304]{2,1,0:T(8,128)} %convert_select_fusion.1, bf16[512,4,192]{0,2,1:T(8,128)(2,1)S(1)} %bitcast.160, f32[4,512]{1,0:T(4,128)S(1)} %rsqrt_bitcast_fusion.4), kind=kOutput, calls=%fused_computation.74 | convolution fusion | flops 7248936960 | bytes 18096128 | tf_op jit(solution)/shard_map/vmap()/dot_general | solution.py:93
  233.9 7.3 %fusion.79 = f32[4,192,768]{2,1,0:T(8,128)} fusion(f32[4,512,1536]{2,1,0:T(8,128)S(1)} %fusion.49, bf16[4,512,192]{1,2,0:T(8,128)(2,1)S(1)} %bitcast.178, f32[4,512]{1,0:T(4,128)S(1)} %get-tuple-element.23), kind=kOutput, calls=%fused_computation.113 | convolution fusion | flops 3633119232 | bytes 15736832 | tf_op jit(solution)/shard_map/vmap()/dot_general | solution.py:101
  241.1 13.6 %add_multiply_fusion.1 = (f32[4,512,768]{2,1,0:T(8,128)}, f32[4,512,768]{2,1,0:T(8,128)}) fusion(f32[4,512,1536]{2,1,0:T(8,128)S(1)} %fusion.49, f32[4,192,2304]{2,1,0:T(8,128)} %convert_select_fusion.1, bf16[4,512,192]{1,2,0:T(8,128)(2,1)S(1)} %bitcast.179, f32[4,512]{1,0:T(4,128)S(1)} %get-tuple-element.23), kind=kOutput, calls=%fused_computation.49 | convolution fusion | flops 3643539456 | bytes 28319744 | tf_op jit(solution)/shard_map/vmap()/dot_general | solution.py:111
  255.3 2.3 copy.15
  257.6 2.3 copy.17
  259.9 2.3 pad_maximum_fusion.1
  262.2 1.5 collective-permute-start
  263.7 1.9 pad_maximum_fusion
  265.6 1.5 collective-permute-start.2
  267.0 11.5 %fusion.4 = f32[4,192,1536]{2,1,0:T(8,128)S(1)} fusion(f32[4,512,768]{2,1,0:T(8,128)} %get-tuple-element.10, f32[4,512,768]{2,1,0:T(8,128)} %get-tuple-element.9, bf16[512,4,192]{0,2,1:T(8,128)(2,1)S(1)} %bitcast.161, f32[4,512]{1,0:T(4,128)S(1)} %rsqrt_bitcast_fusion.4), kind=kOutput, calls=%fused_computation.6 | convolution fusion | flops 7252082688 | bytes 18096128 | tf_op jit(solution)/shard_map/vmap()/dot_general | solution.py:116
  278.6 7.2 %multiply_reduce_fusion.1 = (f32[4,2304]{1,0:T(4,128)S(1)}, f32[4,192,2304]{2,1,0:T(8,128)}, bf16[4,192,2304]{2,1,0:T(8,128)(2,1)}) fusion(f32[4,192,2304]{2,1,0:T(8,128)S(1)} %bitcast.148, f32[4,192,768]{2,1,0:T(8,128)} %fusion.79, f32[4,192,1536]{2,1,0:T(8,128)S(1)} %fusion.4, f32[1,4,192,2304]{3,2,1,0:T(8,128)} %param.12, pred[]{:T(512)} %bitcast.21), kind=kLoop, calls=%fused_computation.27 | loop fusion | flops 14146560 | bytes 31887360 | tf_op jit(solution)/shard_map/vmap()/reduce_sum | solution.py:126
  285.8 5.3 multiply_convert_fusion
  293.7 13.5 %fusion.51 = f32[4,512,1536]{2,1,0:T(8,128)} fusion(f32[4,192,2304]{2,1,0:T(8,128)S(1)} %bitcast.148, bf16[512,4,192]{0,2,1:T(8,128)(2,1)S(1)} %bitcast.169, f32[4,512]{1,0:T(4,128)S(1)} %rsqrt_bitcast_fusion.5), kind=kOutput, calls=%fused_computation.76 | convolution fusion | flops 7248936960 | bytes 18096128 | tf_op jit(solution)/shard_map/vmap()/dot_general | solution.py:81
  307.1 13.6 %fusion.19 = f32[4,512,192]{1,2,0:T(8,128)} fusion(f32[4,512,1536]{2,1,0:T(8,128)} %fusion.51, f32[4,192,2304]{2,1,0:T(8,128)S(1)} %bitcast.148), kind=kOutput, calls=%fused_computation.31 | convolution fusion | flops 3631742976 | bytes 16515072 | tf_op jit(solution)/shard_map/vmap()/dot_general | solution.py:84
  320.8 16.1 %collective-permute-done = bf16[2048,768]{1,0:T(8,128)(2,1)} collective-permute-done((bf16[2048,768]{1,0:T(8,128)(2,1)S(1)}, bf16[2048,768]{1,0:T(8,128)(2,1)}, u32[]{:S(2)}, u32[]{:S(2)}) %collective-permute-start) | collective-permute-done | bytes 3145760 | tf_op jit(solution)/shard_map/ppermute | solution.py:19
  336.9 5.6 copy.16
  342.5 3.7 multiply_reduce_fusion.2
  347.9 8.6 %fusion.60 = f32[4,512,2560]{2,1,0:T(8,128)} fusion(bf16[4,512,192]{1,2,0:T(8,128)(2,1)S(1)} %fusion.103, bf16[4,2048,192]{1,2,0:T(8,128)(2,1)S(1)} %multiply_convert_fusion.1, bf16[512,4,192]{0,2,1:T(8,128)(2,1)S(1)} %bitcast.164, f32[4,512]{1,0:T(4,128)S(1)} %rsqrt_bitcast_fusion.3), kind=kOutput, calls=%fused_computation.85 | convolution fusion | flops 2022309888 | bytes 25698304 | tf_op jit(solution)/shard_map/vmap()/dot_general | solution.py:51
  356.5 22.8 %fusion = (f32[4,512]{1,0:T(4,128)S(1)}, f32[4,512]{1,0:T(4,128)S(1)}, f32[4,512,2560]{2,1,0:T(8,128)}) fusion(f32[2560]{0:T(1024)S(1)} %concatenate.55, pred[512,2560]{1,0:T(8,128)(4,1)} %fusion.44, f32[2560]{0:T(1024)S(1)} %concatenate.60, f32[4,512,2560]{2,1,0:T(8,128)} %fusion.60, bf16[4,512,192]{1,2,0:T(8,128)(2,1)} %fusion.92, ...), kind=kOutput, calls=%fused_computation.2 | convolution fusion | flops 2074734592 | bytes 48017408 | tf_op jit(solution)/shard_map/vmap()/dot_general | solution.py:51
  379.3 11.8 %fusion.108 = bf16[512,4,192]{0,2,1:T(8,128)(2,1)S(1)} fusion(f32[4,512,192]{1,2,0:T(8,128)} %fusion.19, bf16[4,512,192]{1,2,0:T(8,128)(2,1)S(1)} %bitcast.180, bf16[4,2048,192]{1,2,0:T(8,128)(2,1)} %bitcast.171, f32[4,512,2560]{2,1,0:T(8,128)} %get-tuple-element.26, f32[2560]{0:T(1024)S(1)} %concatenate.55, pred[512,2560]{1,0:T(8,128)(4,1)} %fusion.44, ...), kind=kOutput, calls=%fused_computation.135 | convolution fusion | flops 2048917504 | bytes 28592128 | tf_op jit(solution)/shard_map/vmap()/dot_general | solution.py:69
  391.1 6.4 %convolution_convert_fusion.1 = bf16[512,3072]{1,0:T(8,128)(2,1)} fusion(bf16[512,768]{0,1:T(8,128)(2,1)S(1)} %bitcast.181, bf16[768,3072]{1,0:T(8,128)(2,1)} %param.18), kind=kOutput, calls=%fused_computation.69 | convolution fusion | flops 2417491968 | bytes 8650752 | tf_op jit(solution)/shard_map/dot_general | solution.py:179
  397.5 6.8 %collective-permute-done.2 = bf16[2048,768]{1,0:T(8,128)(2,1)} collective-permute-done((bf16[2048,768]{1,0:T(8,128)(2,1)}, bf16[2048,768]{1,0:T(8,128)(2,1)}, u32[]{:S(2)}, u32[]{:S(2)}) %collective-permute-start.2) | collective-permute-done | bytes 3145760 | tf_op jit(solution)/shard_map/ppermute | solution.py:19
  404.3 5.0 copy.18
  409.3 70.8 %collective-permute-done.3 = bf16[4,192,2304]{2,1,0:T(8,128)(2,1)} collective-permute-done((bf16[4,192,2304]{2,1,0:T(8,128)(2,1)}, bf16[4,192,2304]{2,1,0:T(8,128)(2,1)}, u32[]{:S(2)}, u32[]{:S(2)}) %collective-permute-start.3) | collective-permute-done | bytes 3538976 | tf_op jit(solution)/shard_map/ppermute | solution.py:19
  480.1 3.9 convert_select_fusion
  484.0 13.3 %fusion.47 = f32[4,512,1536]{2,1,0:T(8,128)} fusion(f32[4,192,2304]{2,1,0:T(8,128)S(1)} %convert_select_fusion, bf16[512,4,192]{0,2,1:T(8,128)(2,1)S(1)} %bitcast.165, f32[4,512]{1,0:T(4,128)S(1)} %rsqrt_bitcast_fusion.3), kind=kOutput, calls=%fused_computation.72 | convolution fusion | flops 7248936960 | bytes 18096128 | tf_op jit(solution)/shard_map/vmap()/dot_general | solution.py:81
  497.3 13.8 %fusion.18 = f32[4,512,192]{1,2,0:T(8,128)} fusion(f32[4,512,1536]{2,1,0:T(8,128)} %fusion.47, f32[4,192,2304]{2,1,0:T(8,128)S(1)} %convert_select_fusion), kind=kOutput, calls=%fused_computation.29 | convolution fusion | flops 3631742976 | bytes 16515072 | tf_op jit(solution)/shard_map/vmap()/dot_general | solution.py:84
  511.1 12.4 %fusion.107 = bf16[512,4,192]{0,2,1:T(8,128)(2,1)} fusion(f32[4,512,192]{1,2,0:T(8,128)} %fusion.18, bf16[4,512,192]{1,2,0:T(8,128)(2,1)S(1)} %bitcast.175, bf16[4,2048,192]{1,2,0:T(8,128)(2,1)} %bitcast.172, f32[4,512,2560]{2,1,0:T(8,128)} %fusion.60, f32[2560]{0:T(1024)S(1)} %concatenate.60, pred[512,2560]{1,0:T(8,128)(4,1)S(1)} %copy-done.10, ...), kind=kOutput, calls=%fused_computation.132 | convolution fusion | flops 2048917504 | bytes 28592128 | tf_op jit(solution)/shard_map/vmap()/dot_general | solution.py:69
  523.5 6.9 %convolution_convert_fusion = bf16[512,3072]{1,0:T(8,128)(2,1)} fusion(bf16[512,768]{0,1:T(8,128)(2,1)} %bitcast.182, bf16[768,3072]{1,0:T(8,128)(2,1)} %param.18), kind=kOutput, calls=%fused_computation.68 | convolution fusion | flops 2417491968 | bytes 8650752 | tf_op jit(solution)/shard_map/dot_general | solution.py:179
  530.4 13.0 %fusion.45 = f32[4,512,1536]{2,1,0:T(8,128)S(1)} fusion(f32[4,192,2304]{2,1,0:T(8,128)} %copy-done.2, bf16[512,4,192]{0,2,1:T(8,128)(2,1)S(1)} %bitcast.157, f32[4,512]{1,0:T(4,128)S(1)} %rsqrt_bitcast_fusion.2), kind=kOutput, calls=%fused_computation.70 | convolution fusion | flops 7248936960 | bytes 18096128 | tf_op jit(solution)/shard_map/vmap()/dot_general | solution.py:93
  543.4 14.4 %add_multiply_fusion = (f32[4,512,768]{2,1,0:T(8,128)S(1)}, f32[4,512,768]{2,1,0:T(8,128)}) fusion(f32[4,512,1536]{2,1,0:T(8,128)S(1)} %fusion.45, f32[4,192,2304]{2,1,0:T(8,128)} %copy-done.2, bf16[4,512,192]{1,2,0:T(8,128)(2,1)S(1)} %bitcast.176, f32[4,512]{1,0:T(4,128)S(1)} %copy-done.14), kind=kOutput, calls=%fused_computation.38 | convolution fusion | flops 3643539456 | bytes 28319744 | tf_op jit(solution)/shard_map/vmap()/dot_general | solution.py:111
  557.9 10.5 %fusion.8 = f32[4,192,1536]{2,1,0:T(8,128)S(1)} fusion(f32[4,512,768]{2,1,0:T(8,128)} %get-tuple-element.8, f32[4,512,768]{2,1,0:T(8,128)S(1)} %get-tuple-element.7, bf16[512,4,192]{0,2,1:T(8,128)(2,1)S(1)} %bitcast.158, f32[4,512]{1,0:T(4,128)S(1)} %rsqrt_bitcast_fusion.2), kind=kOutput, calls=%fused_computation.10 | convolution fusion | flops 7252082688 | bytes 18096128 | tf_op jit(solution)/shard_map/vmap()/dot_general | solution.py:116
  568.3 9.0 %fusion.82 = f32[4,192,768]{2,1,0:T(8,128)S(1)} fusion(f32[4,512,1536]{2,1,0:T(8,128)} %copy-done.6, bf16[4,512,192]{1,2,0:T(8,128)(2,1)S(1)} %bitcast.177, f32[4,512]{1,0:T(4,128)S(1)} %copy-done.14), kind=kOutput, calls=%fused_computation.114 | convolution fusion | flops 3633119232 | bytes 15736832 | tf_op jit(solution)/shard_map/vmap()/dot_general | solution.py:101
  577.4 4.6 multiply_reduce_fusion
  582.0 8.2 %fusion.71 = (f32[1,4,192,2304]{3,2,1,0:T(8,128)}, f32[1,4,192,2304]{3,2,1,0:T(8,128)}) fusion(f32[4,192,768]{2,1,0:T(8,128)S(1)} %fusion.82, f32[4,192,1536]{2,1,0:T(8,128)S(1)} %fusion.8, bf16[4,192,2304]{2,1,0:T(8,128)(2,1)} %collective-permute-done.4, pred[]{:T(512)} %bitcast.48, f32[4,2304]{1,0:T(4,128)S(1)} %add_rsqrt_fusion, ...), kind=kLoop, calls=%fused_computation.97 | loop fusion | flops 17694720 | bytes 31887360 | tf_op jit(solution)/shard_map/broadcast_in_dim | solution.py:255
  590.3 3.7 pad_maximum_fusion.2
  (77 shorter events, 7.3 us)
Async XLA Ops:
  7.2 33.3 %copy-start = (bf16[3072,4]{0,1:T(4,128)(2,1)S(1)}, bf16[3072,4]{0,1:T(4,128)(2,1)}, u32[]{:S(2)}) copy-start(bf16[3072,4]{0,1:T(4,128)(2,1)} %param.17) | copy-start | bytes 73732
  7.2 33.2 %all-gather.6.cloned.1.call-start = ((), (), s32[]{:S(2)}) async-start(), calls=%async_computation.5 | async-start | bytes 9437184 | tf_op jit(solution)/shard_map/all_gather | solution.py:198
  7.9 191.3 %all-gather.4.cloned.1.call-start = ((), (), s32[]{:S(2)}) async-start(), calls=%async_computation.2 | async-start | bytes 15040512 | tf_op jit(solution)/shard_map/all_gather | solution.py:202
  8.7 581.6 %reduce-scatter.3.cloned.1.call-start = ((), (), s32[]{:S(2)}) async-start(), calls=%async_computation.3 | async-start | bytes 4718592 | tf_op jit(solution)/shard_map/reduce_scatter | solution.py:180
  10.7 29.7 %collective-permute-start.1 = (bf16[2048]{0:T(1024)(128)(2,1)S(1)}, bf16[2048]{0:T(1024)(128)(2,1)S(1)}, u32[]{:S(2)}, u32[]{:S(2)}) collective-permute-start(bf16[2048]{0:T(1024)(128)(2,1)S(1)} %pad_convert_fusion), channel_id=1, source_target_pairs={{30,0},{0,2},{2,4},{4,6},{6,8},{8,10},{10,12},{12,14},{14,16},{16,... | collective-permute-start | bytes 12296 | tf_op jit(solution)/shard_map/ppermute | solution.py:19
  19.9 6.8 %copy-start.4 = (bf16[4,192,2304]{2,1,0:T(8,128)(2,1)S(1)}, bf16[4,192,2304]{2,1,0:T(8,128)(2,1)}, u32[]{:S(2)}) copy-start(bf16[4,192,2304]{2,1,0:T(8,128)(2,1)} %param.13) | copy-start | bytes 10616836
  24.7 8.9 %slice-start.2 = ((s8[6291456]{0:T(1024)(128)(4,1)}), s8[4194304]{0:T(1024)(128)(4,1)S(1)}, s32[]{:S(2)}) async-start(s8[6291456]{0:T(1024)(128)(4,1)} %bitcast.150), calls=%async_computation.8 | async-start | bytes 8388608
  26.7 6.9 %slice-start.3 = ((s8[6291456]{0:T(1024)(128)(4,1)}), s8[2097152]{0:T(1024)(128)(4,1)S(1)}, s32[]{:S(2)}) async-start(s8[6291456]{0:T(1024)(128)(4,1)} %bitcast.150), calls=%async_computation.9 | async-start | bytes 4194304
  33.6 3.8 copy-start.7
  220.5 20.7 %copy-start.12 = (bf16[1,512,768]{1,2,0:T(8,128)(2,1)}, bf16[1,512,768]{1,2,0:T(8,128)(2,1)S(1)}, u32[]{:S(2)}) copy-start(bf16[1,512,768]{1,2,0:T(8,128)(2,1)S(1)} %get-tuple-element.20) | copy-start | bytes 2359300
  259.9 3.8 copy-start.8
  259.9 3.8 copy-start.9
  262.2 74.7 %collective-permute-start = (bf16[2048,768]{1,0:T(8,128)(2,1)S(1)}, bf16[2048,768]{1,0:T(8,128)(2,1)}, u32[]{:S(2)}, u32[]{:S(2)}) collective-permute-start(bf16[2048,768]{1,0:T(8,128)(2,1)S(1)} %pad_maximum_fusion.1), channel_id=1, source_target_pairs={{30,0},{0,2},{2,4},{4,6},{6,8},{8,10},{10,12},{12,14},{14,16},{16,... | collective-permute-start | bytes 9437192 | tf_op jit(solution)/shard_map/ppermute | solution.py:19
  263.7 14.9 %slice-start = ((s8[7077888]{0:T(1024)(128)(4,1)}), s8[4194304]{0:T(1024)(128)(4,1)S(1)}, s32[]{:S(2)}) async-start(s8[7077888]{0:T(1024)(128)(4,1)} %bitcast.147), calls=%async_computation.6 | async-start | bytes 8388608
  265.6 138.8 %collective-permute-start.2 = (bf16[2048,768]{1,0:T(8,128)(2,1)}, bf16[2048,768]{1,0:T(8,128)(2,1)}, u32[]{:S(2)}, u32[]{:S(2)}) collective-permute-start(bf16[2048,768]{1,0:T(8,128)(2,1)} %pad_maximum_fusion), channel_id=1, source_target_pairs={{30,0},{0,2},{2,4},{4,6},{6,8},{8,10},{10,12},{12,14},{14,16},{16,... | collective-permute-start | bytes 9437192 | tf_op jit(solution)/shard_map/ppermute | solution.py:19
  267.0 11.6 %slice-start.1 = ((s8[7077888]{0:T(1024)(128)(4,1)}), s8[2883584]{0:T(1024)(128)(4,1)S(1)}, s32[]{:S(2)}) async-start(s8[7077888]{0:T(1024)(128)(4,1)} %bitcast.147), calls=%async_computation.7 | async-start | bytes 5767168
  291.2 189.0 %collective-permute-start.3 = (bf16[4,192,2304]{2,1,0:T(8,128)(2,1)}, bf16[4,192,2304]{2,1,0:T(8,128)(2,1)}, u32[]{:S(2)}, u32[]{:S(2)}) collective-permute-start(bf16[4,192,2304]{2,1,0:T(8,128)(2,1)} %multiply_convert_fusion), channel_id=1, source_target_pairs={{30,0},{0,2},{2,4},{4,6},{6,8},{8,10},{10,12},{12,14},{14,16},{16,... | collective-permute-start | bytes 10616840 | tf_op jit(solution)/shard_map/ppermute | solution.py:19
  291.9 285.5 %collective-permute-start.4 = (bf16[4,192,2304]{2,1,0:T(8,128)(2,1)}, bf16[4,192,2304]{2,1,0:T(8,128)(2,1)}, u32[]{:S(2)}, u32[]{:S(2)}) collective-permute-start(bf16[4,192,2304]{2,1,0:T(8,128)(2,1)} %get-tuple-element.11), channel_id=1, source_target_pairs={{30,0},{0,2},{2,4},{4,6},{6,8},{8,10},{10,12},{12,14},{14,16},{16,... | collective-permute-start | bytes 10616840 | tf_op jit(solution)/shard_map/ppermute | solution.py:19
  342.5 4.6 copy-start.3
  356.5 22.8 %copy-start.13 = (bf16[1,512,768]{1,2,0:T(8,128)(2,1)S(1)}, bf16[1,512,768]{1,2,0:T(8,128)(2,1)}, u32[]{:S(2)}) copy-start(bf16[1,512,768]{1,2,0:T(8,128)(2,1)} %copy-done.12) | copy-start | bytes 2359300
  397.5 192.8 %reduce-scatter.5.cloned.1.call-start = ((), (), s32[]{:S(2)}) async-start(), calls=%async_computation.4 | async-start | bytes 4718592 | tf_op jit(solution)/shard_map/reduce_scatter | solution.py:180
  484.0 13.3 %copy-start.2 = (f32[4,192,2304]{2,1,0:T(8,128)}, f32[4,192,2304]{2,1,0:T(8,128)S(1)}, u32[]{:S(2)}) copy-start(f32[4,192,2304]{2,1,0:T(8,128)S(1)} %convert_select_fusion) | copy-start | bytes 21233668
  497.3 13.8 %copy-start.10 = (pred[512,2560]{1,0:T(8,128)(4,1)S(1)}, pred[512,2560]{1,0:T(8,128)(4,1)}, u32[]{:S(2)}) copy-start(pred[512,2560]{1,0:T(8,128)(4,1)} %fusion.44) | copy-start | bytes 3932164
  497.3 13.8 %copy-start.11 = (bf16[1,512,768]{1,2,0:T(8,128)(2,1)S(1)}, bf16[1,512,768]{1,2,0:T(8,128)(2,1)}, u32[]{:S(2)}) copy-start(bf16[1,512,768]{1,2,0:T(8,128)(2,1)} %get-tuple-element.17) | copy-start | bytes 2359300
  530.4 13.0 %copy-start.14 = (f32[4,512]{1,0:T(4,128)S(1)}, f32[4,512]{1,0:T(4,128)}, u32[]{:S(2)}) copy-start(f32[4,512]{1,0:T(4,128)} %get-tuple-element.22) | copy-start | bytes 24580
  543.4 14.4 %copy-start.6 = (f32[4,512,1536]{2,1,0:T(8,128)}, f32[4,512,1536]{2,1,0:T(8,128)S(1)}, u32[]{:S(2)}) copy-start(f32[4,512,1536]{2,1,0:T(8,128)S(1)} %fusion.45) | copy-start | bytes 37748740
  568.3 9.0 %copy-start.5 = (bf16[4,192,2304]{2,1,0:T(8,128)(2,1)S(1)}, bf16[4,192,2304]{2,1,0:T(8,128)(2,1)}, u32[]{:S(2)}) copy-start(bf16[4,192,2304]{2,1,0:T(8,128)(2,1)} %param.13) | copy-start | bytes 10616836
  582.0 12.0 %copy-start.1 = (bf16[3072,4]{0,1:T(4,128)(2,1)S(1)}, bf16[3072,4]{0,1:T(4,128)(2,1)}, u32[]{:S(2)}) copy-start(bf16[3072,4]{0,1:T(4,128)(2,1)} %param.17) | copy-start | bytes 73732
Sparse Core Ops, SparseCore 0:
  9.5 19.4 all-gather.5
  31.7 167.4 all-gather.3
  397.6 6.8 reduce-scatter.2
  530.5 6.8 reduce-scatter.4
where the time goes:
time: 610 us; the launch traced here: 601 us
  waiting for transfers between devices  248 us (41%)
  matrix products  240 us (39%)
  other arithmetic  60.5 us (10%)
  local copies, waits for them, and re-layouts  27.6 us (5%)
  between operations  17.2 us (3%)
  starting transfers between devices  7.44 us (1%)
    all_gather x1, waiting for transfers between devices, body(): lax.all_gather(qkv_weight, 'seq', axis=1, tiled=True)  153 us
    ppermute x5, waiting for transfers between devices, passed_along(): return lax.ppermute(block, axis, route)  93.7 us
    dot_general x2, matrix products, head_span(): lax.dot_general(query_unit.astype(jnp.bfloat16), context_keys, (((1,), (1...  31.4 us
    dot_general x2, matrix products, head_span(): jnp.dot(out_grad, down_proj, precision=highest, preferred_element_type=jn...  28 us
    dot_general x2, matrix products, head_span(): lax.dot_general(mixed_hidden, down_proj, (((1,), (1,)), ((), ())), precis...  27.4 us
    dot_general x2, matrix products, head_span(): jnp.dot(query_in, up_proj, precision=highest, preferred_element_type=jnp....  26.7 us
    dot_general x2, matrix products, head_span(): jnp.dot(key_in, up_proj, precision=highest, preferred_element_type=jnp.fl...  26.2 us
    dot_general x2, matrix products, head_span(): jnp.dot(soft_weights.astype(jnp.bfloat16), context_values, preferred_elem...  24.2 us
  transfers between devices with their start and end apart: 9, of which 4 were waited for; matrix products, arithmetic and copies ran while one was open for 43% of the time, Pallas kernels for 0%

commit v1 on v0

--- a/solution.py
+++ b/solution.py
@@ -199,7 +199,7 @@
     projected = jnp.einsum(
         "tr,crh->cth",
         features,
-        lax.all_gather(qkv_weight, "seq", axis=1, tiled=True),
+        jnp.concatenate(lax.all_gather(qkv_weight, "seq"), axis=1),
         preferred_element_type=jnp.float32,
     )
     projected_bf = projected.astype(jnp.bfloat16)

time: 610 us -> 626 us (1.026)
  local copies, waits for them, and re-layouts: 27.6 us -> 40.4 us
    reshape x0 -> x1, local copies, waits for them, and re-layouts: none -> 12.7 us  [body(): jnp.concatenate(lax.all_gather(qkv_weight, 'seq'), axis=1)]
  transfers between devices with their start and end apart: 9 -> 9, of which waited for: 4 -> 4; matrix products, arithmetic and copies ran while one was open for 43% -> 42% of each run, Pallas kernels for 0% -> 0%
where the time goes in v1:
time: 626 us; the launch traced here: 618 us
  waiting for transfers between devices  248 us (40%)
  matrix products  244 us (39%)
  other arithmetic  60.5 us (10%)
  local copies, waits for them, and re-layouts  40.4 us (6%)
  between operations  17.2 us (3%)
  starting transfers between devices  7.57 us (1%)
    all_gather x1, waiting for transfers between devices, body(): lax.all_gather(qkv_weight, 'seq')  153 us
    ppermute x5, waiting for transfers between devices, passed_along(): return lax.ppermute(block, axis, route)  93.8 us
    dot_general x2, matrix products, head_span(): lax.dot_general(query_unit.astype(jnp.bfloat16), context_keys, (((1,), (1...  31.4 us
    dot_general x2, matrix products, head_span(): jnp.dot(out_grad, down_proj, precision=highest, preferred_element_type=jn...  28.5 us
    dot_general x2, matrix products, head_span(): lax.dot_general(mixed_hidden, down_proj, (((1,), (1,)), ((), ())), precis...  27.4 us
    dot_general x2, matrix products, head_span(): jnp.dot(query_in, up_proj, precision=highest, preferred_element_type=jnp....  26.4 us
    dot_general x2, matrix products, head_span(): jnp.dot(key_in, up_proj, precision=highest, preferred_element_type=jnp.fl...  26.4 us
    dot_general x2, matrix products, head_span(): jnp.dot(soft_weights.astype(jnp.bfloat16), context_values, preferred_elem...  24.2 us
  transfers between devices with their start and end apart: 9, of which 4 were waited for; matrix products, arithmetic and copies ran while one was open for 42% of the time, Pallas kernels for 0%

profile of v1, /device:TPU:0, one launch (start us, length us, event | category | flops | bytes accessed | tf_op | source)
XLA Modules:
  0.0 617.6 jit_solution(3801463665782910838)
XLA Ops:
  10.7 3.0 collective-permute-start.1
  14.4 5.5 copy.37
  19.9 4.8 multiply_reduce_fusion.3
  24.7 2.0 fusion.44
  26.7 6.9 %convert_select_fusion.1 = f32[4,192,2304]{2,1,0:T(8,128)} fusion(bf16[4,192,2304]{2,1,0:T(8,128)(2,1)S(1)} %copy-done.4, f32[1,4,192,2304]{3,2,1,0:T(8,128)} %param.11, pred[]{:T(512)} %bitcast.24), kind=kLoop, calls=%fused_computation.19 | loop fusion | flops 3538944 | bytes 17694720 | tf_op jit(solution)/shard_map/vmap(jit(_where))/select_n | solution.py:74
  33.6 2.6 multiply_convert_fusion.2
  37.5 3.0 copy.38
  40.5 5.3 fusion.142
  46.4 152.9 %all-gather.5.cloned.1.call-done = bf16[48,192,768]{2,1,0:T(8,128)(2,1)} async-done(((bf16[3,192,768]{2,1,0:T(8,128)(2,1)}), bf16[48,192,768]{2,1,0:T(8,128)(2,1)}) %all-gather.5.cloned.1.call-update) | async-done | bytes 14155792 | tf_op jit(solution)/shard_map/all_gather | solution.py:202
  199.3 12.7 %copy.35 = bf16[3,16,192,768]{3,2,1,0:T(8,128)(2,1)} copy(bf16[3,16,192,768]{3,2,0,1:T(8,128)(2,1)} %bitcast.172) | data formatting | bytes 28311552 | tf_op jit(solution)/shard_map/reshape | solution.py:202
  212.0 18.0 %convert_bitcast_fusion = bf16[3,1024,768]{1,2,0:T(8,128)(2,1)S(1)} fusion(bf16[3,3072,768]{2,1,0:T(8,128)(2,1)} %bitcast.173, bf16[1,1024,3072]{2,1,0:T(8,128)(2,1)S(1)} %bitcast.180), kind=kOutput, calls=%fused_computation.67 | convolution fusion | flops 14497873920 | bytes 25165824 | tf_op jit(solution)/shard_map/tr,crh->cth/dot_general | solution.py:199
  230.1 1.8 fusion.168
  232.1 13.4 %fusion.49 = f32[4,512,1536]{2,1,0:T(8,128)} fusion(f32[4,192,2304]{2,1,0:T(8,128)S(1)} %bitcast.152, bf16[512,4,192]{0,2,1:T(8,128)(2,1)S(1)} %bitcast.166, f32[4,512]{1,0:T(4,128)S(1)} %rsqrt_bitcast_fusion.4), kind=kOutput, calls=%fused_computation.74 | convolution fusion | flops 7248936960 | bytes 18096128 | tf_op jit(solution)/shard_map/vmap()/dot_general | solution.py:93
  245.5 11.8 %fusion.79 = f32[4,192,768]{2,1,0:T(8,128)} fusion(f32[4,512,1536]{2,1,0:T(8,128)} %fusion.49, bf16[4,512,192]{1,2,0:T(8,128)(2,1)S(1)} %bitcast.188, f32[4,512]{1,0:T(4,128)S(1)} %get-tuple-element.23), kind=kOutput, calls=%fused_computation.113 | convolution fusion | flops 3633119232 | bytes 15736832 | tf_op jit(solution)/shard_map/vmap()/dot_general | solution.py:101
  257.3 14.0 %add_multiply_fusion.1 = (f32[4,512,768]{2,1,0:T(8,128)}, f32[4,512,768]{2,1,0:T(8,128)}) fusion(f32[4,512,1536]{2,1,0:T(8,128)} %fusion.49, f32[4,192,2304]{2,1,0:T(8,128)S(1)} %bitcast.152, bf16[4,512,192]{1,2,0:T(8,128)(2,1)S(1)} %bitcast.189, f32[4,512]{1,0:T(4,128)S(1)} %get-tuple-element.23), kind=kOutput, calls=%fused_computation.49 | convolution fusion | flops 3643539456 | bytes 28319744 | tf_op jit(solution)/shard_map/vmap()/dot_general | solution.py:111
  271.9 2.3 copy.39
  274.2 2.3 copy.41
  276.5 2.3 pad_maximum_fusion.1
  278.7 1.5 collective-permute-start
  280.2 1.9 pad_maximum_fusion
  282.1 1.5 collective-permute-start.2
  283.6 11.5 %fusion.4 = f32[4,192,1536]{2,1,0:T(8,128)S(1)} fusion(f32[4,512,768]{2,1,0:T(8,128)} %get-tuple-element.10, f32[4,512,768]{2,1,0:T(8,128)} %get-tuple-element.9, bf16[512,4,192]{0,2,1:T(8,128)(2,1)S(1)} %bitcast.167, f32[4,512]{1,0:T(4,128)S(1)} %rsqrt_bitcast_fusion.4), kind=kOutput, calls=%fused_computation.6 | convolution fusion | flops 7252082688 | bytes 18096128 | tf_op jit(solution)/shard_map/vmap()/dot_general | solution.py:116
  295.2 7.2 %multiply_reduce_fusion.1 = (f32[4,2304]{1,0:T(4,128)S(1)}, f32[4,192,2304]{2,1,0:T(8,128)}, bf16[4,192,2304]{2,1,0:T(8,128)(2,1)}) fusion(f32[4,192,2304]{2,1,0:T(8,128)S(1)} %bitcast.154, f32[4,192,768]{2,1,0:T(8,128)} %fusion.79, f32[4,192,1536]{2,1,0:T(8,128)S(1)} %fusion.4, f32[1,4,192,2304]{3,2,1,0:T(8,128)} %param.12, pred[]{:T(512)} %bitcast.24), kind=kLoop, calls=%fused_computation.27 | loop fusion | flops 14146560 | bytes 31887360 | tf_op jit(solution)/shard_map/vmap()/reduce_sum | solution.py:126
  302.4 5.3 multiply_convert_fusion
  310.4 13.2 %fusion.51 = f32[4,512,1536]{2,1,0:T(8,128)} fusion(f32[4,192,2304]{2,1,0:T(8,128)S(1)} %bitcast.154, bf16[512,4,192]{0,2,1:T(8,128)(2,1)S(1)} %bitcast.177, f32[4,512]{1,0:T(4,128)S(1)} %rsqrt_bitcast_fusion.5), kind=kOutput, calls=%fused_computation.76 | convolution fusion | flops 7248936960 | bytes 18096128 | tf_op jit(solution)/shard_map/vmap()/dot_general | solution.py:81
  323.6 13.7 %fusion.19 = f32[4,512,192]{1,2,0:T(8,128)} fusion(f32[4,512,1536]{2,1,0:T(8,128)} %fusion.51, f32[4,192,2304]{2,1,0:T(8,128)S(1)} %bitcast.154), kind=kOutput, calls=%fused_computation.31 | convolution fusion | flops 3631742976 | bytes 16515072 | tf_op jit(solution)/shard_map/vmap()/dot_general | solution.py:84
  337.3 16.2 %collective-permute-done = bf16[2048,768]{1,0:T(8,128)(2,1)} collective-permute-done((bf16[2048,768]{1,0:T(8,128)(2,1)S(1)}, bf16[2048,768]{1,0:T(8,128)(2,1)}, u32[]{:S(2)}, u32[]{:S(2)}) %collective-permute-start) | collective-permute-done | bytes 3145760 | tf_op jit(solution)/shard_map/ppermute | solution.py:19
  353.5 5.6 copy.40
  359.0 3.7 multiply_reduce_fusion.2
  364.5 8.6 %fusion.60 = f32[4,512,2560]{2,1,0:T(8,128)} fusion(bf16[4,512,192]{1,2,0:T(8,128)(2,1)S(1)} %fusion.103, bf16[4,2048,192]{1,2,0:T(8,128)(2,1)S(1)} %multiply_convert_fusion.1, bf16[512,4,192]{0,2,1:T(8,128)(2,1)S(1)} %bitcast.170, f32[4,512]{1,0:T(4,128)S(1)} %rsqrt_bitcast_fusion.3), kind=kOutput, calls=%fused_computation.85 | convolution fusion | flops 2022309888 | bytes 25698304 | tf_op jit(solution)/shard_map/vmap()/dot_general | solution.py:51
  373.1 22.8 %fusion = (f32[4,512]{1,0:T(4,128)S(1)}, f32[4,512]{1,0:T(4,128)S(1)}, f32[4,512,2560]{2,1,0:T(8,128)}) fusion(f32[2560]{0:T(1024)S(1)} %concatenate.55, pred[512,2560]{1,0:T(8,128)(4,1)} %fusion.44, f32[2560]{0:T(1024)S(1)} %concatenate.60, f32[4,512,2560]{2,1,0:T(8,128)} %fusion.60, bf16[4,512,192]{1,2,0:T(8,128)(2,1)} %fusion.92, ...), kind=kOutput, calls=%fused_computation.2 | convolution fusion | flops 2074734592 | bytes 48017408 | tf_op jit(solution)/shard_map/vmap()/dot_general | solution.py:51
  395.9 11.8 %fusion.108 = bf16[512,4,192]{0,2,1:T(8,128)(2,1)S(1)} fusion(f32[4,512,192]{1,2,0:T(8,128)} %fusion.19, bf16[4,512,192]{1,2,0:T(8,128)(2,1)S(1)} %bitcast.190, bf16[4,2048,192]{1,2,0:T(8,128)(2,1)} %bitcast.181, f32[4,512,2560]{2,1,0:T(8,128)} %get-tuple-element.26, f32[2560]{0:T(1024)S(1)} %concatenate.55, pred[512,2560]{1,0:T(8,128)(4,1)} %fusion.44, ...), kind=kOutput, calls=%fused_computation.135 | convolution fusion | flops 2048917504 | bytes 28592128 | tf_op jit(solution)/shard_map/vmap()/dot_general | solution.py:69
  407.6 6.4 %convolution_convert_fusion.1 = bf16[512,3072]{1,0:T(8,128)(2,1)} fusion(bf16[512,768]{0,1:T(8,128)(2,1)S(1)} %bitcast.191, bf16[768,3072]{1,0:T(8,128)(2,1)} %param.18), kind=kOutput, calls=%fused_computation.69 | convolution fusion | flops 2417491968 | bytes 8650752 | tf_op jit(solution)/shard_map/dot_general | solution.py:179
  414.1 6.8 %collective-permute-done.2 = bf16[2048,768]{1,0:T(8,128)(2,1)} collective-permute-done((bf16[2048,768]{1,0:T(8,128)(2,1)}, bf16[2048,768]{1,0:T(8,128)(2,1)}, u32[]{:S(2)}, u32[]{:S(2)}) %collective-permute-start.2) | collective-permute-done | bytes 3145760 | tf_op jit(solution)/shard_map/ppermute | solution.py:19
  420.9 5.0 copy.42
  425.9 70.8 %collective-permute-done.3 = bf16[4,192,2304]{2,1,0:T(8,128)(2,1)} collective-permute-done((bf16[4,192,2304]{2,1,0:T(8,128)(2,1)}, bf16[4,192,2304]{2,1,0:T(8,128)(2,1)}, u32[]{:S(2)}, u32[]{:S(2)}) %collective-permute-start.3) | collective-permute-done | bytes 3538976 | tf_op jit(solution)/shard_map/ppermute | solution.py:19
  496.7 3.9 convert_select_fusion
  500.6 13.2 %fusion.47 = f32[4,512,1536]{2,1,0:T(8,128)} fusion(f32[4,192,2304]{2,1,0:T(8,128)S(1)} %convert_select_fusion, bf16[512,4,192]{0,2,1:T(8,128)(2,1)S(1)} %bitcast.171, f32[4,512]{1,0:T(4,128)S(1)} %rsqrt_bitcast_fusion.3), kind=kOutput, calls=%fused_computation.72 | convolution fusion | flops 7248936960 | bytes 18096128 | tf_op jit(solution)/shard_map/vmap()/dot_general | solution.py:81
  513.8 13.8 %fusion.18 = f32[4,512,192]{1,2,0:T(8,128)} fusion(f32[4,512,1536]{2,1,0:T(8,128)} %fusion.47, f32[4,192,2304]{2,1,0:T(8,128)S(1)} %convert_select_fusion), kind=kOutput, calls=%fused_computation.29 | convolution fusion | flops 3631742976 | bytes 16515072 | tf_op jit(solution)/shard_map/vmap()/dot_general | solution.py:84
  527.6 12.5 %fusion.107 = bf16[512,4,192]{0,2,1:T(8,128)(2,1)} fusion(f32[4,512,192]{1,2,0:T(8,128)} %fusion.18, bf16[4,512,192]{1,2,0:T(8,128)(2,1)S(1)} %bitcast.185, bf16[4,2048,192]{1,2,0:T(8,128)(2,1)} %bitcast.182, f32[4,512,2560]{2,1,0:T(8,128)} %fusion.60, f32[2560]{0:T(1024)S(1)} %concatenate.60, pred[512,2560]{1,0:T(8,128)(4,1)S(1)} %copy-done.10, ...), kind=kOutput, calls=%fused_computation.132 | convolution fusion | flops 2048917504 | bytes 28592128 | tf_op jit(solution)/shard_map/vmap()/dot_general | solution.py:69
  540.1 6.9 %convolution_convert_fusion = bf16[512,3072]{1,0:T(8,128)(2,1)} fusion(bf16[512,768]{0,1:T(8,128)(2,1)} %bitcast.192, bf16[768,3072]{1,0:T(8,128)(2,1)} %param.18), kind=kOutput, calls=%fused_computation.68 | convolution fusion | flops 2417491968 | bytes 8650752 | tf_op jit(solution)/shard_map/dot_general | solution.py:179
  547.0 13.0 %fusion.45 = f32[4,512,1536]{2,1,0:T(8,128)S(1)} fusion(f32[4,192,2304]{2,1,0:T(8,128)} %copy-done.2, bf16[512,4,192]{0,2,1:T(8,128)(2,1)S(1)} %bitcast.163, f32[4,512]{1,0:T(4,128)S(1)} %rsqrt_bitcast_fusion.2), kind=kOutput, calls=%fused_computation.70 | convolution fusion | flops 7248936960 | bytes 18096128 | tf_op jit(solution)/shard_map/vmap()/dot_general | solution.py:93
  560.0 14.4 %add_multiply_fusion = (f32[4,512,768]{2,1,0:T(8,128)S(1)}, f32[4,512,768]{2,1,0:T(8,128)}) fusion(f32[4,512,1536]{2,1,0:T(8,128)S(1)} %fusion.45, f32[4,192,2304]{2,1,0:T(8,128)} %copy-done.2, bf16[4,512,192]{1,2,0:T(8,128)(2,1)S(1)} %bitcast.186, f32[4,512]{1,0:T(4,128)S(1)} %copy-done.14), kind=kOutput, calls=%fused_computation.38 | convolution fusion | flops 3643539456 | bytes 28319744 | tf_op jit(solution)/shard_map/vmap()/dot_general | solution.py:111
  574.4 10.5 %fusion.8 = f32[4,192,1536]{2,1,0:T(8,128)S(1)} fusion(f32[4,512,768]{2,1,0:T(8,128)} %get-tuple-element.8, f32[4,512,768]{2,1,0:T(8,128)S(1)} %get-tuple-element.7, bf16[512,4,192]{0,2,1:T(8,128)(2,1)S(1)} %bitcast.164, f32[4,512]{1,0:T(4,128)S(1)} %rsqrt_bitcast_fusion.2), kind=kOutput, calls=%fused_computation.10 | convolution fusion | flops 7252082688 | bytes 18096128 | tf_op jit(solution)/shard_map/vmap()/dot_general | solution.py:116
  584.9 9.0 %fusion.82 = f32[4,192,768]{2,1,0:T(8,128)S(1)} fusion(f32[4,512,1536]{2,1,0:T(8,128)} %copy-done.6, bf16[4,512,192]{1,2,0:T(8,128)(2,1)S(1)} %bitcast.187, f32[4,512]{1,0:T(4,128)S(1)} %copy-done.14), kind=kOutput, calls=%fused_computation.114 | convolution fusion | flops 3633119232 | bytes 15736832 | tf_op jit(solution)/shard_map/vmap()/dot_general | solution.py:101
  593.9 4.6 multiply_reduce_fusion
  598.6 8.2 %fusion.71 = (f32[1,4,192,2304]{3,2,1,0:T(8,128)}, f32[1,4,192,2304]{3,2,1,0:T(8,128)}) fusion(f32[4,192,768]{2,1,0:T(8,128)S(1)} %fusion.82, f32[4,192,1536]{2,1,0:T(8,128)S(1)} %fusion.8, bf16[4,192,2304]{2,1,0:T(8,128)(2,1)} %collective-permute-done.4, pred[]{:T(512)} %bitcast.51, f32[4,2304]{1,0:T(4,128)S(1)} %add_rsqrt_fusion, ...), kind=kLoop, calls=%fused_computation.97 | loop fusion | flops 17694720 | bytes 31887360 | tf_op jit(solution)/shard_map/broadcast_in_dim | solution.py:255
  606.8 3.7 pad_maximum_fusion.2
  (88 shorter events, 8.8 us)
Async XLA Ops:
  7.2 33.3 %copy-start = (bf16[3072,4]{0,1:T(4,128)(2,1)S(1)}, bf16[3072,4]{0,1:T(4,128)(2,1)}, u32[]{:S(2)}) copy-start(bf16[3072,4]{0,1:T(4,128)(2,1)} %param.17) | copy-start | bytes 73732
  7.2 33.3 %all-gather.7.cloned.1.call-start = ((), (), s32[]{:S(2)}) async-start(), calls=%async_computation.5 | async-start | bytes 9437184 | tf_op jit(solution)/shard_map/all_gather | solution.py:198
  7.9 191.4 %all-gather.5.cloned.1.call-start = ((), (), s32[]{:S(2)}) async-start(), calls=%async_computation.4 | async-start | bytes 15040512 | tf_op jit(solution)/shard_map/all_gather | solution.py:202
  8.7 598.2 %reduce-scatter.3.cloned.1.call-start = ((), (), s32[]{:S(2)}) async-start(), calls=%async_computation.2 | async-start | bytes 4718592 | tf_op jit(solution)/shard_map/reduce_scatter | solution.py:180
  10.7 29.7 %collective-permute-start.1 = (bf16[2048]{0:T(1024)(128)(2,1)S(1)}, bf16[2048]{0:T(1024)(128)(2,1)S(1)}, u32[]{:S(2)}, u32[]{:S(2)}) collective-permute-start(bf16[2048]{0:T(1024)(128)(2,1)S(1)} %pad_convert_fusion), channel_id=1, source_target_pairs={{30,0},{0,2},{2,4},{4,6},{6,8},{8,10},{10,12},{12,14},{14,16},{16,... | collective-permute-start | bytes 12296 | tf_op jit(solution)/shard_map/ppermute | solution.py:19
  19.9 6.8 %copy-start.4 = (bf16[4,192,2304]{2,1,0:T(8,128)(2,1)S(1)}, bf16[4,192,2304]{2,1,0:T(8,128)(2,1)}, u32[]{:S(2)}) copy-start(bf16[4,192,2304]{2,1,0:T(8,128)(2,1)} %param.13) | copy-start | bytes 10616836
  24.7 8.9 %slice-start.4 = ((s8[6291456]{0:T(1024)(128)(4,1)}), s8[4194304]{0:T(1024)(128)(4,1)S(1)}, s32[]{:S(2)}) async-start(s8[6291456]{0:T(1024)(128)(4,1)} %bitcast.156), calls=%async_computation.10 | async-start | bytes 8388608
  26.7 6.9 %slice-start.5 = ((s8[6291456]{0:T(1024)(128)(4,1)}), s8[2097152]{0:T(1024)(128)(4,1)S(1)}, s32[]{:S(2)}) async-start(s8[6291456]{0:T(1024)(128)(4,1)} %bitcast.156), calls=%async_computation.11 | async-start | bytes 4194304
  33.6 3.9 copy-start.7
  40.5 171.5 %slice-start.6 = ((s8[6291456]{0:T(1024)(128)(4,1)}), s8[2097152]{0:T(1024)(128)(4,1)S(1)}, s32[]{:S(2)}) async-start(s8[6291456]{0:T(1024)(128)(4,1)} %bitcast.179), calls=%async_computation.12 | async-start | bytes 4194304
  199.3 12.7 %slice-start.7 = ((s8[6291456]{0:T(1024)(128)(4,1)}), s8[4194304]{0:T(1024)(128)(4,1)S(1)}, s32[]{:S(2)}) async-start(s8[6291456]{0:T(1024)(128)(4,1)} %bitcast.179), calls=%async_computation.13 | async-start | bytes 8388608
  199.3 32.7 %slice-start = ((s8[7077888]{0:T(1024)(128)(4,1)}), s8[4194304]{0:T(1024)(128)(4,1)S(1)}, s32[]{:S(2)}) async-start(s8[7077888]{0:T(1024)(128)(4,1)} %bitcast.151), calls=%async_computation.6 | async-start | bytes 8388608
  212.0 20.0 %slice-start.1 = ((s8[7077888]{0:T(1024)(128)(4,1)}), s8[2883584]{0:T(1024)(128)(4,1)S(1)}, s32[]{:S(2)}) async-start(s8[7077888]{0:T(1024)(128)(4,1)} %bitcast.151), calls=%async_computation.7 | async-start | bytes 5767168
  231.8 25.5 %copy-start.12 = (bf16[1,512,768]{1,2,0:T(8,128)(2,1)}, bf16[1,512,768]{1,2,0:T(8,128)(2,1)S(1)}, u32[]{:S(2)}) copy-start(bf16[1,512,768]{1,2,0:T(8,128)(2,1)S(1)} %get-tuple-element.20) | copy-start | bytes 2359300
  276.5 3.8 copy-start.8
  276.5 3.8 copy-start.9
  278.7 74.7 %collective-permute-start = (bf16[2048,768]{1,0:T(8,128)(2,1)S(1)}, bf16[2048,768]{1,0:T(8,128)(2,1)}, u32[]{:S(2)}, u32[]{:S(2)}) collective-permute-start(bf16[2048,768]{1,0:T(8,128)(2,1)S(1)} %pad_maximum_fusion.1), channel_id=1, source_target_pairs={{30,0},{0,2},{2,4},{4,6},{6,8},{8,10},{10,12},{12,14},{14,16},{16,... | collective-permute-start | bytes 9437192 | tf_op jit(solution)/shard_map/ppermute | solution.py:19
  280.2 14.9 %slice-start.2 = ((s8[7077888]{0:T(1024)(128)(4,1)}), s8[4194304]{0:T(1024)(128)(4,1)S(1)}, s32[]{:S(2)}) async-start(s8[7077888]{0:T(1024)(128)(4,1)} %bitcast.153), calls=%async_computation.8 | async-start | bytes 8388608
  282.1 138.8 %collective-permute-start.2 = (bf16[2048,768]{1,0:T(8,128)(2,1)}, bf16[2048,768]{1,0:T(8,128)(2,1)}, u32[]{:S(2)}, u32[]{:S(2)}) collective-permute-start(bf16[2048,768]{1,0:T(8,128)(2,1)} %pad_maximum_fusion), channel_id=1, source_target_pairs={{30,0},{0,2},{2,4},{4,6},{6,8},{8,10},{10,12},{12,14},{14,16},{16,... | collective-permute-start | bytes 9437192 | tf_op jit(solution)/shard_map/ppermute | solution.py:19
  283.6 11.6 %slice-start.3 = ((s8[7077888]{0:T(1024)(128)(4,1)}), s8[2883584]{0:T(1024)(128)(4,1)S(1)}, s32[]{:S(2)}) async-start(s8[7077888]{0:T(1024)(128)(4,1)} %bitcast.153), calls=%async_computation.9 | async-start | bytes 5767168
  307.7 189.0 %collective-permute-start.3 = (bf16[4,192,2304]{2,1,0:T(8,128)(2,1)}, bf16[4,192,2304]{2,1,0:T(8,128)(2,1)}, u32[]{:S(2)}, u32[]{:S(2)}) collective-permute-start(bf16[4,192,2304]{2,1,0:T(8,128)(2,1)} %multiply_convert_fusion), channel_id=1, source_target_pairs={{30,0},{0,2},{2,4},{4,6},{6,8},{8,10},{10,12},{12,14},{14,16},{16,... | collective-permute-start | bytes 10616840 | tf_op jit(solution)/shard_map/ppermute | solution.py:19
  308.4 285.5 %collective-permute-start.4 = (bf16[4,192,2304]{2,1,0:T(8,128)(2,1)}, bf16[4,192,2304]{2,1,0:T(8,128)(2,1)}, u32[]{:S(2)}, u32[]{:S(2)}) collective-permute-start(bf16[4,192,2304]{2,1,0:T(8,128)(2,1)} %get-tuple-element.11), channel_id=1, source_target_pairs={{30,0},{0,2},{2,4},{4,6},{6,8},{8,10},{10,12},{12,14},{14,16},{16,... | collective-permute-start | bytes 10616840 | tf_op jit(solution)/shard_map/ppermute | solution.py:19
  359.0 4.6 copy-start.3
  373.1 22.8 %copy-start.13 = (bf16[1,512,768]{1,2,0:T(8,128)(2,1)S(1)}, bf16[1,512,768]{1,2,0:T(8,128)(2,1)}, u32[]{:S(2)}) copy-start(bf16[1,512,768]{1,2,0:T(8,128)(2,1)} %copy-done.12) | copy-start | bytes 2359300
  414.1 192.8 %reduce-scatter.5.cloned.1.call-start = ((), (), s32[]{:S(2)}) async-start(), calls=%async_computation.3 | async-start | bytes 4718592 | tf_op jit(solution)/shard_map/reduce_scatter | solution.py:180
  500.6 13.2 %copy-start.2 = (f32[4,192,2304]{2,1,0:T(8,128)}, f32[4,192,2304]{2,1,0:T(8,128)S(1)}, u32[]{:S(2)}) copy-start(f32[4,192,2304]{2,1,0:T(8,128)S(1)} %convert_select_fusion) | copy-start | bytes 21233668
  513.8 13.8 %copy-start.10 = (pred[512,2560]{1,0:T(8,128)(4,1)S(1)}, pred[512,2560]{1,0:T(8,128)(4,1)}, u32[]{:S(2)}) copy-start(pred[512,2560]{1,0:T(8,128)(4,1)} %fusion.44) | copy-start | bytes 3932164
  513.8 13.8 %copy-start.11 = (bf16[1,512,768]{1,2,0:T(8,128)(2,1)S(1)}, bf16[1,512,768]{1,2,0:T(8,128)(2,1)}, u32[]{:S(2)}) copy-start(bf16[1,512,768]{1,2,0:T(8,128)(2,1)} %get-tuple-element.17) | copy-start | bytes 2359300
  547.0 13.0 %copy-start.14 = (f32[4,512]{1,0:T(4,128)S(1)}, f32[4,512]{1,0:T(4,128)}, u32[]{:S(2)}) copy-start(f32[4,512]{1,0:T(4,128)} %get-tuple-element.22) | copy-start | bytes 24580
  560.0 14.4 %copy-start.6 = (f32[4,512,1536]{2,1,0:T(8,128)}, f32[4,512,1536]{2,1,0:T(8,128)S(1)}, u32[]{:S(2)}) copy-start(f32[4,512,1536]{2,1,0:T(8,128)S(1)} %fusion.45) | copy-start | bytes 37748740
  584.9 9.0 %copy-start.5 = (bf16[4,192,2304]{2,1,0:T(8,128)(2,1)S(1)}, bf16[4,192,2304]{2,1,0:T(8,128)(2,1)}, u32[]{:S(2)}) copy-start(bf16[4,192,2304]{2,1,0:T(8,128)(2,1)} %param.13) | copy-start | bytes 10616836
  598.6 12.0 %copy-start.1 = (bf16[3072,4]{0,1:T(4,128)(2,1)S(1)}, bf16[3072,4]{0,1:T(4,128)(2,1)}, u32[]{:S(2)}) copy-start(bf16[3072,4]{0,1:T(4,128)(2,1)} %param.17) | copy-start | bytes 73732
Sparse Core Ops, SparseCore 0:
  9.5 19.4 all-gather.6
  31.8 167.4 all-gather.4
  414.2 6.8 reduce-scatter.2
  547.1 6.8 reduce-scatter.4
